TPU v7x, 128 devices: a whole 4x4x4 slice. The times are simulated.
128 devices in a mesh: segment: 8 (over y, x_hi), tp: 16 (over x_lo, z, core).
Axes of the slice: x: 4 (x_hi: 2, x_lo: 2; x = x_hi * 2 + x_lo), y: 4, z: 4, core: 2. Of those that a mesh axis runs over, the one named last changes fastest.
Arguments:
- memory: bfloat16 [1024, 4096], P('segment', 'tp'), may hold values from -6 to 6
- norm_gain: float32 [4096], replicated, may hold values from 0.1 to 1.9
- queries: bfloat16 [8, 1024, 4096], P('segment', None, 'tp'), may hold values from -200 to 200
- key_weight: bfloat16 [8, 4096, 4096], P('segment', None, 'tp'), may hold values from -0.09375 to 0.09375
- value_weight: bfloat16 [8, 4096, 4096], P('segment', None, 'tp'), may hold values from -0.09375 to 0.09375
- context_grad: bfloat16 [8, 1024, 4096], P('segment', None, 'tp'), may hold values from -6 to 6
Outputs:
- context: bfloat16 [8, 1024, 4096], P('segment', None, 'tp')
- query_grad: bfloat16 [8, 1024, 4096], P('segment', None, 'tp')
- key_weight_grad: float32 [8, 4096, 4096], P('segment', None, 'tp')
- value_weight_grad: float32 [8, 4096, 4096], P('segment', None, 'tp')
- encoder_output_gradient: float32 [1024, 4096], P('segment', 'tp')
All inputs are finite; a program needn't handle non-finite values.
Results may differ from a plain program's by a relative error of at most 0.015.
The roundings to bfloat16 on the way count: a program that leaves them out, or rounds other values in their place, can miss the bound.
Values may be sent and summed in bfloat16 or wider, within the bound.
No kernel may reach another device: no remote copies, remote signals or barrier semaphores. Data moves between devices by JAX's collectives and lax.ppermute only.
A program may use at most 128 MiB of HBM per device.

v0:
```python
import jax
import jax.numpy as jnp
from jax import lax
from jax.sharding import PartitionSpec as P

HD = 256


def joined_along(pieces, dim):
    pieces = jnp.moveaxis(pieces, 0, dim)
    shape = pieces.shape
    return pieces.reshape(*shape[:dim], shape[dim] * shape[dim + 1], *shape[dim + 2 :])


def sent_to_all(value, axis):
    copies = jnp.broadcast_to(value, (lax.axis_size(axis), *value.shape))
    return lax.all_to_all(copies, axis, split_axis=0, concat_axis=0, tiled=True)


def collect(value, axis, dim):
    return joined_along(sent_to_all(value, axis), dim)


def of_everyone(value, axis):
    return sent_to_all(value, axis).sum(axis=0)


def in_blocks(value, dim, size):
    before, after = (value.shape[:dim], value.shape[dim + 1 :])
    return jnp.moveaxis(value.reshape(*before, size, -1, *after), dim, 0)


def summed_on_arrival(value, axis, dim):
    size = lax.axis_size(axis)
    pieces = lax.all_to_all(in_blocks(value, dim, size), axis, 0, 0, tiled=True)
    return jnp.sum(pieces.astype(jnp.float32), axis=0)


def local(memory, norm_gain, queries, key_weight, value_weight, context_grad):
    epsilon_value = 1e-06
    hidden_width = norm_gain.shape[0]
    piece_cols = memory.shape[1]
    rows_own = memory.shape[0]
    tp_index = lax.axis_index("tp")
    segment_index = lax.axis_index("segment")
    own_gain = lax.dynamic_slice_in_dim(norm_gain, tp_index * piece_cols, piece_cols)
    local_row_block = memory.astype(jnp.float32)
    gathered = collect(memory, "segment", 0)
    source_all = gathered.astype(jnp.float32)
    squares = of_everyone(jnp.sum(source_all * source_all, axis=1), "tp")
    scale_all = lax.rsqrt(squares / hidden_width + epsilon_value)
    normed_piece = (source_all * scale_all[:, None] * own_gain).astype(jnp.bfloat16)
    normed = lax.all_gather(normed_piece, "tp", axis=1, tiled=True)
    local_scale = lax.dynamic_slice_in_dim(scale_all, segment_index * rows_own, rows_own)
    key_mat = key_weight[0]
    value_mat = value_weight[0]
    query_rows = queries[0]
    dctx = context_grad[0]
    source_count = normed.shape[0]
    target_count = query_rows.shape[0]
    head_count = key_mat.shape[1] // HD
    scale = HD ** (-0.5)
    key_rows = jnp.dot(normed, key_mat, preferred_element_type=jnp.float32).astype(jnp.bfloat16)
    value_rows = jnp.dot(normed, value_mat, preferred_element_type=jnp.float32).astype(jnp.bfloat16)
    qh = query_rows.reshape(target_count, head_count, HD)
    kh = key_rows.reshape(source_count, head_count, HD)
    vh = value_rows.reshape(source_count, head_count, HD)
    dch = dctx.reshape(target_count, head_count, HD)
    scores = jnp.einsum("qhd,khd->hqk", qh, kh, preferred_element_type=jnp.float32) * scale
    maxima = jnp.max(scores, axis=-1, keepdims=True)
    exponent = jnp.exp(scores - maxima)
    attend = exponent / jnp.sum(exponent, axis=-1, keepdims=True)
    attend_low = attend.astype(jnp.bfloat16)
    context = jnp.einsum("hqk,khd->qhd", attend_low, vh, preferred_element_type=jnp.float32).astype(
        jnp.bfloat16
    )
    grad_attend = jnp.einsum("qhd,khd->hqk", dch, vh, preferred_element_type=jnp.float32)
    row_dots = jnp.sum(grad_attend * attend, axis=-1, keepdims=True)
    grad_scores = (attend * (grad_attend - row_dots) * scale).astype(jnp.bfloat16)
    query_grad = jnp.einsum(
        "hqk,khd->qhd", grad_scores, kh, preferred_element_type=jnp.float32
    ).astype(jnp.bfloat16)
    grad_keys = jnp.einsum(
        "hqk,qhd->khd", grad_scores, qh, preferred_element_type=jnp.float32
    ).astype(jnp.bfloat16)
    grad_values = jnp.einsum(
        "hqk,qhd->khd", attend_low, dch, preferred_element_type=jnp.float32
    ).astype(jnp.bfloat16)
    grad_keys = grad_keys.reshape(source_count, head_count * HD)
    grad_values = grad_values.reshape(source_count, head_count * HD)
    key_grad = jnp.einsum("sd,sc->dc", normed, grad_keys, preferred_element_type=jnp.float32)
    value_grad = jnp.einsum("sd,sc->dc", normed, grad_values, preferred_element_type=jnp.float32)
    total = jnp.einsum("sc,dc->sd", grad_keys, key_mat, preferred_element_type=jnp.float32)
    segment_part = lax.psum_scatter(
        (
            total
            + jnp.einsum("sc,dc->sd", grad_values, value_mat, preferred_element_type=jnp.float32)
        ).astype(jnp.bfloat16),
        "segment",
        scatter_dimension=0,
        tiled=True,
    )
    summed = summed_on_arrival(segment_part, "tp", 1)
    upper_term = summed * own_gain
    centered_normalized = local_row_block * local_scale[:, None]
    inner_product = of_everyone(jnp.sum(upper_term * centered_normalized, axis=1), "tp")
    encoder_output_gradient = local_scale[:, None] * (
        upper_term - centered_normalized * (inner_product / hidden_width)[:, None]
    )
    return (
        context.reshape(1, target_count, head_count * HD),
        query_grad.reshape(1, target_count, head_count * HD),
        key_grad[None],
        value_grad[None],
        encoder_output_gradient,
    )


def solution(mesh):
    placed = (
        P("segment", "tp"),
        P(),
        P("segment", None, "tp"),
        P("segment", None, "tp"),
        P("segment", None, "tp"),
        P("segment", None, "tp"),
    )
    return jax.shard_map(
        local,
        mesh=mesh,
        in_specs=placed,
        out_specs=(
            P("segment", None, "tp"),
            P("segment", None, "tp"),
            P("segment", None, "tp"),
            P("segment", None, "tp"),
            P("segment", "tp"),
        ),
        check_vma=False,
    )
```

profile of v0, /device:TPU:1, one launch (start us, length us, event | category | flops | bytes accessed | tf_op | source)
XLA Modules:
  0.0 292.4 jit_solution(10155391424537069540)
XLA Ops:
  7.2 0.0 copy-start
  7.2 1.0 broadcast_in_dim.12
  8.2 18.0 %all_to_all.22 = bf16[8,128,256]{2,1,0:T(8,128)(2,1)S(1)} all-to-all(bf16[8,128,256]{2,1,0:T(8,128)(2,1)S(1)} %broadcast_in_dim.12), channel_id=1, replica_groups=mesh['segment'=8,'tp'=16] {'segment'}, dimensions={0} | all-to-all | bytes 1048576 | tf_op jit(solution)/shard_map/all_to_all | solution.py:17
  26.2 0.2 multiply_reduce_fusion.1
  26.4 0.7 broadcast_in_dim.28
  27.0 7.2 %all-to-all-start.1 = ((f32[16,1,1024]{2,1,0:T(1,128)}), f32[16,1,1024]{2,1,0:T(1,128)S(1)}, u32[]{:S(2)}, u32[]{:S(2)}) async-start(f32[16,1,1024]{2,1,0:T(1,128)} %broadcast_in_dim.28), calls=%async_computation.1 | async-start | bytes 131072 | tf_op jit(solution)/shard_map/all_to_all | solution.py:17
  34.3 0.0 all-gather.2.cloned.1.call-start
  34.3 0.8 dynamic_slice.6
  35.1 5.0 %all-to-all-done.1 = f32[16,1,1024]{2,1,0:T(1,128)S(1)} async-done(((f32[16,1,1024]{2,1,0:T(1,128)}), f32[16,1,1024]{2,1,0:T(1,128)S(1)}, u32[]{:S(2)}, u32[]{:S(2)}) %all-to-all-start.1) | async-done | bytes 65568 | tf_op jit(solution)/shard_map/all_to_all | solution.py:17
  40.1 0.1 reduce_sum.64
  40.2 1.0 fusion.22
  41.2 0.0 all-gather.2.cloned.1.call-update
  41.2 0.0 reduce-scatter.2.cloned.1.call-start
  41.2 57.2 %all-gather.2.cloned.1.call-done = bf16[1024,4096]{1,0:T(8,128)(2,1)} async-done(((bf16[1024,256]{1,0:T(8,128)(2,1)}), bf16[1024,4096]{1,0:T(8,128)(2,1)}) %all-gather.2.cloned.1.call-update) | async-done | bytes 8388624 | tf_op jit(solution)/shard_map/all_gather | solution.py:53
  98.4 5.7 %fusion.16 = bf16[1024,256]{1,0:T(8,128)(2,1)S(1)} fusion(bf16[1024,4096]{1,0:T(8,128)(2,1)} %all-gather.2.cloned.1.call-done, bf16[1,4096,256]{2,1,0:T(8,128)(2,1)S(1)} %copy-done), kind=kOutput, calls=%fused_computation.23 | convolution fusion | flops 2147745792 | bytes 11010048 | tf_op jit(solution)/shard_map/dot_general | solution.py:63
  104.1 0.0 copy-start.4
  104.1 0.0 copy-start.10
  104.2 0.8 multiply_reduce_fusion
  104.9 0.7 fusion.5
  105.7 0.0 copy-start.5
  105.7 1.0 convolution_convert_fusion
  106.7 2.0 slice-done
  108.7 0.6 copy-done.5
  109.3 1.2 slice-done.1
  110.5 2.3 fusion.13
  112.9 1.5 fusion
  114.4 1.3 fusion.3
  115.7 1.3 copy-done.3
  117.0 0.7 convolution_convert_fusion.1
  117.7 8.1 %fusion.6 = f32[1024,4096]{1,0:T(8,128)} fusion(bf16[1024,256]{1,0:T(8,128)(2,1)S(1)} %convolution_convert_fusion.1, bf16[1,4096,256]{2,1,0:T(8,128)(2,1)S(1)} %copy-done), kind=kOutput, calls=%fused_computation.14 | convolution fusion | flops 2147483648 | bytes 19398656 | tf_op jit(solution)/shard_map/sc,dc->sd/dot_general | solution.py:93
  125.8 11.6 %add_convert_fusion = bf16[1024,4096]{1,0:T(8,128)(2,1)} fusion(f32[1024,4096]{1,0:T(8,128)} %fusion.6, bf16[1024,256]{1,0:T(8,128)(2,1)S(1)} %convolution_convert_fusion, bf16[1,4096,256]{2,1,0:T(8,128)(2,1)S(1)} %copy-done.5), kind=kOutput, calls=%fused_computation | convolution fusion | flops 2155872256 | bytes 27787264 | tf_op jit(solution)/shard_map/sc,dc->sd/dot_general | solution.py:97
  137.4 0.0 reduce-scatter.2.cloned.1.call-update
  137.4 0.1 dynamic_slice.7
  137.5 7.8 %convolution_bitcast_fusion.1 = f32[1,4096,256]{2,1,0:T(8,128)} fusion(bf16[1024,4096]{1,0:T(8,128)(2,1)} %all-gather.2.cloned.1.call-done, bf16[1024,256]{1,0:T(8,128)(2,1)S(1)} %convolution_convert_fusion.1), kind=kOutput, calls=%fused_computation.2 | convolution fusion | flops 2147483648 | bytes 13107200 | tf_op jit(solution)/shard_map/sd,sc->dc/dot_general | solution.py:91
  145.3 104.9 %reduce-scatter.2.cloned.1.call-done = bf16[128,4096]{1,0:T(8,128)(2,1)} async-done(((bf16[1024,4096]{1,0:T(8,128)(2,1)}), bf16[128,4096]{1,0:T(8,128)(2,1)}) %reduce-scatter.2.cloned.1.call-update) | async-done | bytes 1048592 | tf_op jit(solution)/shard_map/reduce_scatter | solution.py:94
  250.2 2.4 copy.31
  252.6 5.7 %all-to-all-start.2 = ((bf16[16,128,256]{2,1,0:T(8,128)(2,1)}), bf16[16,128,256]{2,1,0:T(8,128)(2,1)S(1)}, u32[]{:S(2)}, u32[]{:S(2)}) async-start(bf16[16,128,256]{2,1,0:T(8,128)(2,1)} %bitcast.89), calls=%async_computation.3 | async-start | bytes 2097152 | tf_op jit(solution)/shard_map/all_to_all | solution.py:35
  258.3 4.2 %fusion.19 = bf16[1,1024,256]{1,2,0:T(8,128)(2,1)} fusion(bf16[1024,256]{1,0:T(8,128)(2,1)S(1)} %copy-done.12, f32[1024,1024]{1,0:T(8,128)} %copy-done.2, f32[1024]{0:T(1024)S(1)} %fusion.5, f32[1024]{0:T(1024)S(1)} %get-tuple-element.25), kind=kOutput, calls=%fused_computation.28 | convolution fusion | flops 541327360 | bytes 5251072 | tf_op jit(solution)/shard_map/hqk,khd->qhd/dot_general | solution.py:74
  262.5 8.0 %convolution_bitcast_fusion = f32[1,4096,256]{2,1,0:T(8,128)} fusion(bf16[1024,4096]{1,0:T(8,128)(2,1)} %all-gather.2.cloned.1.call-done, bf16[1024,256]{1,0:T(8,128)(2,1)S(1)} %copy-done.9), kind=kOutput, calls=%fused_computation.1 | convolution fusion | flops 2147483648 | bytes 13107200 | tf_op jit(solution)/shard_map/sd,sc->dc/dot_general | solution.py:92
  270.5 3.6 %all-to-all-done.2 = bf16[16,128,256]{2,1,0:T(8,128)(2,1)S(1)} async-done(((bf16[16,128,256]{2,1,0:T(8,128)(2,1)}), bf16[16,128,256]{2,1,0:T(8,128)(2,1)S(1)}, u32[]{:S(2)}, u32[]{:S(2)}) %all-to-all-start.2) | async-done | bytes 1048608 | tf_op jit(solution)/shard_map/all_to_all | solution.py:35
  274.1 0.1 convert_reduce_fusion
  274.3 0.2 multiply_reduce_fusion.2
  274.5 0.6 broadcast_in_dim.31
  275.1 4.1 %all-to-all-start.3 = ((f32[16,1,128]{2,1,0:T(1,128)}), f32[16,1,128]{2,1,0:T(1,128)S(1)}, u32[]{:S(2)}, u32[]{:S(2)}) async-start(f32[16,1,128]{2,1,0:T(1,128)} %broadcast_in_dim.31), calls=%async_computation.4 | async-start | bytes 16384 | tf_op jit(solution)/shard_map/all_to_all | solution.py:17
  279.2 2.5 fusion.20
  281.7 2.0 copy.26
  283.7 1.0 copy.27
  284.8 0.8 subtract_multiply_fusion
  (27 shorter events, 0.1 us)
Async XLA Ops:
  7.2 91.2 %copy-start = (bf16[1,4096,256]{2,1,0:T(8,128)(2,1)S(1)}, bf16[1,4096,256]{2,1,0:T(8,128)(2,1)}, u32[]{:S(2)}) copy-start(bf16[1,4096,256]{2,1,0:T(8,128)(2,1)} %param.9) | copy-start | bytes 6291460
  27.0 13.0 %all-to-all-start.1 = ((f32[16,1,1024]{2,1,0:T(1,128)}), f32[16,1,1024]{2,1,0:T(1,128)S(1)}, u32[]{:S(2)}, u32[]{:S(2)}) async-start(f32[16,1,1024]{2,1,0:T(1,128)} %broadcast_in_dim.28), calls=%async_computation.1 | async-start | bytes 131072 | tf_op jit(solution)/shard_map/all_to_all | solution.py:17
  34.3 64.1 %all-gather.2.cloned.1.call-start = ((), (), s32[]{:S(2)}) async-start(), calls=%async_computation.5 | async-start | bytes 8912896 | tf_op jit(solution)/shard_map/all_gather | solution.py:53
  41.2 62.9 %copy-start.7 = (bf16[1,1024,256]{2,1,0:T(8,128)(2,1)S(1)}, bf16[1,1024,256]{2,1,0:T(8,128)(2,1)}, u32[]{:S(2)}) copy-start(bf16[1,1024,256]{2,1,0:T(8,128)(2,1)} %param.8) | copy-start | bytes 1572868
  41.2 209.0 %reduce-scatter.2.cloned.1.call-start = ((), (), s32[]{:S(2)}) async-start(), calls=%async_computation.6 | async-start | bytes 9437184 | tf_op jit(solution)/shard_map/reduce_scatter | solution.py:94
  104.1 1.5 copy-start.4
  104.1 1.5 copy-start.10
  104.9 9.5 %copy-start.2 = (f32[1024,1024]{1,0:T(8,128)}, f32[1024,1024]{1,0:T(8,128)S(1)}, u32[]{:S(2)}) copy-start(f32[1024,1024]{1,0:T(8,128)S(1)} %get-tuple-element.26) | copy-start | bytes 12582916
  104.9 3.7 %slice-start = ((s8[8388608]{0:T(1024)(128)(4,1)}), s8[4194304]{0:T(1024)(128)(4,1)S(1)}, s32[]{:S(2)}) async-start(s8[8388608]{0:T(1024)(128)(4,1)} %bitcast.93), calls=%async_computation.7 | async-start | bytes 8388608
  105.7 3.6 %copy-start.5 = (bf16[1,4096,256]{2,1,0:T(8,128)(2,1)S(1)}, bf16[1,4096,256]{2,1,0:T(8,128)(2,1)}, u32[]{:S(2)}) copy-start(bf16[1,4096,256]{2,1,0:T(8,128)(2,1)} %param.10) | copy-start | bytes 6291460
  105.7 4.8 %slice-start.1 = ((s8[8388608]{0:T(1024)(128)(4,1)}), s8[4194304]{0:T(1024)(128)(4,1)S(1)}, s32[]{:S(2)}) async-start(s8[8388608]{0:T(1024)(128)(4,1)} %bitcast.93), calls=%async_computation.8 | async-start | bytes 8388608
  110.5 15.3 %copy-start.8 = (bf16[1024,256]{1,0:T(8,128)(2,1)}, bf16[1024,256]{1,0:T(8,128)(2,1)S(1)}, u32[]{:S(2)}) copy-start(bf16[1024,256]{1,0:T(8,128)(2,1)S(1)} %convolution_convert_fusion) | copy-start | bytes 1572868
  112.8 1.5 copy-start.11
  115.7 1.3 copy-start.3
  145.3 113.0 %copy-start.12 = (bf16[1024,256]{1,0:T(8,128)(2,1)S(1)}, bf16[1024,256]{1,0:T(8,128)(2,1)}, u32[]{:S(2)}) copy-start(bf16[1024,256]{1,0:T(8,128)(2,1)} %copy-done.11) | copy-start | bytes 1572868
  252.6 21.5 %all-to-all-start.2 = ((bf16[16,128,256]{2,1,0:T(8,128)(2,1)}), bf16[16,128,256]{2,1,0:T(8,128)(2,1)S(1)}, u32[]{:S(2)}, u32[]{:S(2)}) async-start(bf16[16,128,256]{2,1,0:T(8,128)(2,1)} %bitcast.89), calls=%async_computation.3 | async-start | bytes 2097152 | tf_op jit(solution)/shard_map/all_to_all | solution.py:35
  258.3 4.2 %copy-start.9 = (bf16[1024,256]{1,0:T(8,128)(2,1)S(1)}, bf16[1024,256]{1,0:T(8,128)(2,1)}, u32[]{:S(2)}) copy-start(bf16[1024,256]{1,0:T(8,128)(2,1)} %copy-done.8) | copy-start | bytes 1572868
  262.5 11.8 %copy-start.6 = (bf16[128,256]{1,0:T(8,128)(2,1)S(1)}, bf16[128,256]{1,0:T(8,128)(2,1)}, u32[]{:S(2)}) copy-start(bf16[128,256]{1,0:T(8,128)(2,1)} %param.6) | copy-start | bytes 196612
  262.5 23.1 %copy-start.1 = (bf16[1,4096,256]{2,1,0:T(8,128)(2,1)S(1)}, bf16[1,4096,256]{2,1,0:T(8,128)(2,1)}, u32[]{:S(2)}) copy-start(bf16[1,4096,256]{2,1,0:T(8,128)(2,1)} %param.9) | copy-start | bytes 6291460
  275.1 9.7 %all-to-all-start.3 = ((f32[16,1,128]{2,1,0:T(1,128)}), f32[16,1,128]{2,1,0:T(1,128)S(1)}, u32[]{:S(2)}, u32[]{:S(2)}) async-start(f32[16,1,128]{2,1,0:T(1,128)} %broadcast_in_dim.31), calls=%async_computation.4 | async-start | bytes 16384 | tf_op jit(solution)/shard_map/all_to_all | solution.py:17
Sparse Core Ops, SparseCore 0:
  41.3 57.0 all-gather.1
  137.5 112.6 reduce-scatter.1
where the time goes:
time: 293 us; the launch traced here: 292 us
  waiting for transfers between devices  171 us (58%)
  matrix products  54.2 us (18%)
  blocking collectives  18 us (6%)
  starting transfers between devices  17.1 us (6%)
  between operations  14.3 us (5%)
  local copies, waits for them, and re-layouts  13.8 us (5%)
  other arithmetic  4.37 us (1%)
    reduce_scatter x1, waiting for transfers between devices, local(): lax.psum_scatter((total + jnp.einsum('sc,dc->sd', grad_values, value_mat,...  105 us
    all_gather x1, waiting for transfers between devices, local(): normed = lax.all_gather(normed_piece, 'tp', axis=1, tiled=True)  57.2 us
    all_to_all x1, blocking collectives, sent_to_all(): return lax.all_to_all(copies, axis, split_axis=0, concat_axis=0, tiled=True)  18 us
    dot_general x1, matrix products, local(): jnp.einsum('sc,dc->sd', grad_values, value_mat, preferred_element_type=jn...  11.6 us
    all_to_all x2, starting transfers between devices, sent_to_all(): return lax.all_to_all(copies, axis, split_axis=0, concat_axis=0, tiled=True)  11.3 us
    unnamed x32, local copies, waits for them, and re-layouts  8.26 us
    dot_general x1, matrix products, local(): jnp.einsum('sc,dc->sd', grad_keys, key_mat, preferred_element_type=jnp.fl...  8.1 us
    dot_general x1, matrix products, local(): jnp.einsum('sd,sc->dc', normed, grad_values, preferred_element_type=jnp.f...  8.01 us
  transfers between devices with their start and end apart: 5, of which 4 were waited for; matrix products, arithmetic and copies ran while one was open for 9% of the time, Pallas kernels for 0%

commit v1 on v0

--- a/solution.py
+++ b/solution.py
@@ -50,7 +50,9 @@
     squares = of_everyone(jnp.sum(source_all * source_all, axis=1), "tp")
     scale_all = lax.rsqrt(squares / hidden_width + epsilon_value)
     normed_piece = (source_all * scale_all[:, None] * own_gain).astype(jnp.bfloat16)
-    normed = lax.all_gather(normed_piece, "tp", axis=1, tiled=True)
+    normed = jnp.concatenate(
+        lax.all_to_all(jnp.stack([normed_piece] * lax.axis_size("tp")), "tp", 0, 0), axis=1
+    )
     local_scale = lax.dynamic_slice_in_dim(scale_all, segment_index * rows_own, rows_own)
     key_mat = key_weight[0]
     value_mat = value_weight[0]

time: 293 us -> 326 us (1.11)
  blocking collectives: 18 us -> 115 us
  waiting for transfers between devices: 171 us -> 113 us
  matrix products: 54.2 us -> 48.1 us
    all_to_all x0 -> x1, blocking collectives: none -> 97.1 us  [local(): lax.all_to_all(jnp.stack([normed_piece] * lax.axis_size('tp')), 'tp', 0, 0)]
    all_gather x1 -> x0, waiting for transfers between devices: 57.2 us -> none  [local(): normed = lax.all_gather(normed_piece, 'tp', axis=1, tiled=True)]
    reduce_scatter x1, waiting for transfers between devices: 105 us -> 102 us  [local(): lax.psum_scatter((total + jnp.einsum('sc,dc->sd', grad_values, value_mat,...]
    dot_general x1, matrix products: 5.7 us -> 2.42 us  [local(): jnp.dot(normed, key_mat, preferred_element_type=jnp.float32)]
    unnamed x32 -> x31, local copies, waits for them, and re-layouts: 8.26 us -> 7.53 us
  transfers between devices with their start and end apart: 5 -> 4, of which waited for: 4 -> 4; matrix products, arithmetic and copies ran while one was open for 9% -> 7% of each run, Pallas kernels for 0% -> 0%
where the time goes in v1:
time: 326 us
  blocking collectives  115 us (35%)
  waiting for transfers between devices  113 us (35%)
  matrix products  48.1 us (15%)
  starting transfers between devices  17.1 us (5%)
  between operations  14.3 us (4%)
  local copies, waits for them, and re-layouts  13.6 us (4%)
  other arithmetic  4.81 us (1%)
    reduce_scatter x1, waiting for transfers between devices, local(): lax.psum_scatter((total + jnp.einsum('sc,dc->sd', grad_values, value_mat,...  102 us
    all_to_all x1, blocking collectives, local(): lax.all_to_all(jnp.stack([normed_piece] * lax.axis_size('tp')), 'tp', 0, 0)  97.1 us
    all_to_all x1, blocking collectives, sent_to_all(): return lax.all_to_all(copies, axis, split_axis=0, concat_axis=0, tiled=True)  18 us
    dot_general x1, matrix products, local(): jnp.einsum('sc,dc->sd', grad_values, value_mat, preferred_element_type=jn...  11.4 us
    all_to_all x2, starting transfers between devices, sent_to_all(): return lax.all_to_all(copies, axis, split_axis=0, concat_axis=0, tiled=True)  11.3 us
    dot_general x1, matrix products, local(): jnp.einsum('sc,dc->sd', grad_keys, key_mat, preferred_element_type=jnp.fl...  8.1 us
    dot_general x1, matrix products, local(): jnp.einsum('sd,sc->dc', normed, grad_values, preferred_element_type=jnp.f...  7.89 us
    dot_general x1, matrix products, local(): jnp.einsum('sd,sc->dc', normed, grad_keys, preferred_element_type=jnp.flo...  7.74 us
  transfers between devices with their start and end apart: 4, of which 4 were waited for; matrix products, arithmetic and copies ran while one was open for 7% of the time, Pallas kernels for 0%

profile of v1, /device:TPU:1, one launch (start us, length us, event | category | flops | bytes accessed | tf_op | source)
XLA Modules:
  0.0 325.7 jit_solution(2254289203654126806)
XLA Ops:
  7.2 0.0 copy-start
  7.2 1.1 copy.37
  8.3 0.1 broadcast_in_dim.12
  8.4 18.0 %all_to_all.27 = bf16[8,128,256]{1,2,0:T(8,128)(2,1)S(1)} all-to-all(bf16[8,128,256]{1,2,0:T(8,128)(2,1)S(1)} %broadcast_in_dim.12), channel_id=1, replica_groups=mesh['segment'=8,'tp'=16] {'segment'}, dimensions={0} | all-to-all | bytes 1048576 | tf_op jit(solution)/shard_map/all_to_all | solution.py:17
  26.3 0.2 copy.38
  26.5 0.2 multiply_reduce_fusion.1
  26.8 0.7 broadcast_in_dim.28
  27.4 7.2 %all-to-all-start.1 = ((f32[16,1,1024]{2,1,0:T(1,128)}), f32[16,1,1024]{2,1,0:T(1,128)S(1)}, u32[]{:S(2)}, u32[]{:S(2)}) async-start(f32[16,1,1024]{2,1,0:T(1,128)} %broadcast_in_dim.28), calls=%async_computation.1 | async-start | bytes 131072 | tf_op jit(solution)/shard_map/all_to_all | solution.py:17
  34.6 0.0 reduce-scatter.2.cloned.1.call-start
  34.7 0.8 dynamic_slice.6
  35.5 5.0 %all-to-all-done.1 = f32[16,1,1024]{2,1,0:T(1,128)S(1)} async-done(((f32[16,1,1024]{2,1,0:T(1,128)}), f32[16,1,1024]{2,1,0:T(1,128)S(1)}, u32[]{:S(2)}, u32[]{:S(2)}) %all-to-all-start.1) | async-done | bytes 65568 | tf_op jit(solution)/shard_map/all_to_all | solution.py:17
  40.5 0.1 reduce_sum.64
  40.5 0.2 fusion.22
  40.7 0.2 copy.40
  41.0 1.1 stack.2
  42.1 97.1 %all_to_all.28 = bf16[16,1024,256]{1,2,0:T(8,128)(2,1)S(1)} all-to-all(bf16[16,1024,256]{1,2,0:T(8,128)(2,1)S(1)} %stack.2), channel_id=1, replica_groups=mesh['segment'=8,'tp'=16] {'tp'}, dimensions={0} | all-to-all | bytes 16777216 | tf_op jit(solution)/shard_map/all_to_all | solution.py:54
  139.2 2.4 fusion.16
  141.6 1.1 copy-done.2
  142.7 2.4 fusion.13
  145.1 0.0 copy-start.13
  145.1 0.8 multiply_reduce_fusion
  145.9 0.7 fusion.5
  146.7 1.0 convolution_convert_fusion
  147.6 1.5 fusion
  149.1 1.3 fusion.3
  150.4 1.3 copy-done.5
  151.7 0.7 convolution_convert_fusion.1
  152.4 8.1 %fusion.6 = f32[1024,4096]{1,0:T(8,128)} fusion(bf16[1024,256]{1,0:T(8,128)(2,1)S(1)} %convolution_convert_fusion.1, bf16[1,4096,256]{2,1,0:T(8,128)(2,1)S(1)} %copy-done), kind=kOutput, calls=%fused_computation.14 | convolution fusion | flops 2147483648 | bytes 19398656 | tf_op jit(solution)/shard_map/sc,dc->sd/dot_general | solution.py:95
  160.5 11.4 %add_convert_fusion = bf16[1024,4096]{1,0:T(8,128)(2,1)} fusion(f32[1024,4096]{1,0:T(8,128)} %fusion.6, bf16[1024,256]{1,0:T(8,128)(2,1)S(1)} %convolution_convert_fusion, bf16[1,4096,256]{2,1,0:T(8,128)(2,1)S(1)} %copy-done.6), kind=kOutput, calls=%fused_computation | convolution fusion | flops 2155872256 | bytes 27787264 | tf_op jit(solution)/shard_map/sc,dc->sd/dot_general | solution.py:99
  171.9 0.0 reduce-scatter.2.cloned.1.call-update
  172.0 0.1 dynamic_slice.7
  172.0 0.9 copy-done.10
  173.0 7.7 %convolution_bitcast_fusion.1 = f32[1,4096,256]{2,1,0:T(8,128)} fusion(bf16[1024,4096]{0,1:T(8,128)(2,1)} %bitcast.95, bf16[1024,256]{1,0:T(8,128)(2,1)S(1)} %copy-done.10), kind=kOutput, calls=%fused_computation.2 | convolution fusion | flops 2147483648 | bytes 13107200 | tf_op jit(solution)/shard_map/sd,sc->dc/dot_general | solution.py:93
  180.7 101.5 %reduce-scatter.2.cloned.1.call-done = bf16[128,4096]{1,0:T(8,128)(2,1)} async-done(((bf16[1024,4096]{1,0:T(8,128)(2,1)}), bf16[128,4096]{1,0:T(8,128)(2,1)}) %reduce-scatter.2.cloned.1.call-update) | async-done | bytes 1048592 | tf_op jit(solution)/shard_map/reduce_scatter | solution.py:96
  282.2 2.4 copy.49
  284.6 5.7 %all-to-all-start.3 = ((bf16[16,128,256]{2,1,0:T(8,128)(2,1)}), bf16[16,128,256]{2,1,0:T(8,128)(2,1)}, u32[]{:S(2)}, u32[]{:S(2)}) async-start(bf16[16,128,256]{2,1,0:T(8,128)(2,1)} %bitcast.92), calls=%async_computation.4 | async-start | bytes 2097152 | tf_op jit(solution)/shard_map/all_to_all | solution.py:35
  290.4 7.9 %convolution_bitcast_fusion = f32[1,4096,256]{2,1,0:T(8,128)} fusion(bf16[1024,4096]{0,1:T(8,128)(2,1)} %bitcast.96, bf16[1024,256]{1,0:T(8,128)(2,1)S(1)} %convolution_convert_fusion), kind=kOutput, calls=%fused_computation.1 | convolution fusion | flops 2147483648 | bytes 13107200 | tf_op jit(solution)/shard_map/sd,sc->dc/dot_general | solution.py:94
  298.3 1.9 fusion.19
  300.2 6.1 %all-to-all-done.3 = bf16[16,128,256]{2,1,0:T(8,128)(2,1)} async-done(((bf16[16,128,256]{2,1,0:T(8,128)(2,1)}), bf16[16,128,256]{2,1,0:T(8,128)(2,1)}, u32[]{:S(2)}, u32[]{:S(2)}) %all-to-all-start.3) | async-done | bytes 1048608 | tf_op jit(solution)/shard_map/all_to_all | solution.py:35
  306.3 1.4 convert_reduce_fusion
  307.7 0.2 multiply_reduce_fusion.2
  307.9 0.6 broadcast_in_dim.31
  308.5 4.1 %all-to-all-start.4 = ((f32[16,1,128]{2,1,0:T(1,128)}), f32[16,1,128]{2,1,0:T(1,128)S(1)}, u32[]{:S(2)}, u32[]{:S(2)}) async-start(f32[16,1,128]{2,1,0:T(1,128)} %broadcast_in_dim.31), calls=%async_computation.5 | async-start | bytes 16384 | tf_op jit(solution)/shard_map/all_to_all | solution.py:17
  312.6 2.3 fusion.20
  314.9 2.0 copy.44
  317.0 1.0 copy.45
  318.0 0.1 all-to-all-done.4
  318.1 0.8 subtract_multiply_fusion
  (26 shorter events, 0.1 us)
Async XLA Ops:
  7.2 132.0 %copy-start = (bf16[1,4096,256]{2,1,0:T(8,128)(2,1)S(1)}, bf16[1,4096,256]{2,1,0:T(8,128)(2,1)}, u32[]{:S(2)}) copy-start(bf16[1,4096,256]{2,1,0:T(8,128)(2,1)} %param.9) | copy-start | bytes 6291460
  27.4 13.0 %all-to-all-start.1 = ((f32[16,1,1024]{2,1,0:T(1,128)}), f32[16,1,1024]{2,1,0:T(1,128)S(1)}, u32[]{:S(2)}, u32[]{:S(2)}) async-start(f32[16,1,1024]{2,1,0:T(1,128)} %broadcast_in_dim.28), calls=%async_computation.1 | async-start | bytes 131072 | tf_op jit(solution)/shard_map/all_to_all | solution.py:17
  34.6 247.6 %reduce-scatter.2.cloned.1.call-start = ((), (), s32[]{:S(2)}) async-start(), calls=%async_computation.6 | async-start | bytes 9437184 | tf_op jit(solution)/shard_map/reduce_scatter | solution.py:96
  139.2 3.5 %copy-start.2 = (bf16[16,1024,256]{1,2,0:T(8,128)(2,1)}, bf16[16,1024,256]{1,2,0:T(8,128)(2,1)S(1)}, u32[]{:S(2)}) copy-start(bf16[16,1024,256]{1,2,0:T(8,128)(2,1)S(1)} %all_to_all.28) | copy-start | bytes 25165828
  139.2 3.5 %copy-start.6 = (bf16[1,4096,256]{2,1,0:T(8,128)(2,1)S(1)}, bf16[1,4096,256]{2,1,0:T(8,128)(2,1)}, u32[]{:S(2)}) copy-start(bf16[1,4096,256]{2,1,0:T(8,128)(2,1)} %param.10) | copy-start | bytes 6291460
  142.7 2.4 copy-start.8
  145.1 2.5 copy-start.11
  145.1 1.5 copy-start.13
  145.9 3.2 copy-start.3
  150.4 1.3 copy-start.5
  152.4 8.1 %copy-start.9 = (bf16[1024,256]{1,0:T(8,128)(2,1)}, bf16[1024,256]{1,0:T(8,128)(2,1)S(1)}, u32[]{:S(2)}) copy-start(bf16[1024,256]{1,0:T(8,128)(2,1)S(1)} %convolution_convert_fusion.1) | copy-start | bytes 1572868
  171.9 1.0 copy-start.10
  284.6 21.7 %all-to-all-start.3 = ((bf16[16,128,256]{2,1,0:T(8,128)(2,1)}), bf16[16,128,256]{2,1,0:T(8,128)(2,1)}, u32[]{:S(2)}, u32[]{:S(2)}) async-start(bf16[16,128,256]{2,1,0:T(8,128)(2,1)} %bitcast.92), calls=%async_computation.4 | async-start | bytes 2097152 | tf_op jit(solution)/shard_map/all_to_all | solution.py:35
  290.4 7.9 %copy-start.4 = (f32[1024,1024]{1,0:T(8,128)S(1)}, f32[1024,1024]{1,0:T(8,128)}, u32[]{:S(2)}) copy-start(f32[1024,1024]{1,0:T(8,128)} %copy-done.3) | copy-start | bytes 12582916
  290.4 7.9 %copy-start.12 = (bf16[1024,256]{1,0:T(8,128)(2,1)S(1)}, bf16[1024,256]{1,0:T(8,128)(2,1)}, u32[]{:S(2)}) copy-start(bf16[1024,256]{1,0:T(8,128)(2,1)} %copy-done.11) | copy-start | bytes 1572868
  298.3 9.4 %copy-start.7 = (bf16[128,256]{1,0:T(8,128)(2,1)S(1)}, bf16[128,256]{1,0:T(8,128)(2,1)}, u32[]{:S(2)}) copy-start(bf16[128,256]{1,0:T(8,128)(2,1)} %param.6) | copy-start | bytes 196612
  298.3 20.6 %copy-start.1 = (bf16[1,4096,256]{2,1,0:T(8,128)(2,1)S(1)}, bf16[1,4096,256]{2,1,0:T(8,128)(2,1)}, u32[]{:S(2)}) copy-start(bf16[1,4096,256]{2,1,0:T(8,128)(2,1)} %param.9) | copy-start | bytes 6291460
  308.5 9.6 %all-to-all-start.4 = ((f32[16,1,128]{2,1,0:T(1,128)}), f32[16,1,128]{2,1,0:T(1,128)S(1)}, u32[]{:S(2)}, u32[]{:S(2)}) async-start(f32[16,1,128]{2,1,0:T(1,128)} %broadcast_in_dim.31), calls=%async_computation.5 | async-start | bytes 16384 | tf_op jit(solution)/shard_map/all_to_all | solution.py:17
Sparse Core Ops, SparseCore 0:
  172.1 110.1 reduce-scatter.1
